TPU v7x, 512 devices: a whole 4x4x16 slice. The times are simulated.
512 devices in a mesh: tm: 16 (over z_hi, y, core), seq: 32 (over x, z_lo).
Axes of the slice: x: 4, y: 4, z: 16 (z_hi: 2, z_lo: 8; z = z_hi * 8 + z_lo), core: 2. Of those that a mesh axis runs over, the one named last changes fastest.
Arguments:
- queries: bfloat16 [16, 768, 4096], P('tm', 'seq'), may hold values from -144 to 144
- keys_proj: bfloat16 [16, 768, 4096], P('tm', 'seq'), may hold values from -12 to 12
- values: bfloat16 [16, 768, 4096], P('tm', 'seq'), may hold values from -4 to 4
- hidden: bfloat16 [16, 768, 4096], P('tm', 'seq'), may hold values from -4 to 4
- fresh_latent: bfloat16 [768, 4096], P('seq'), may hold values from -4 to 4
- gate_table: float32 [50, 4096], replicated, may hold values from 0.5 to 2.5
- noise_step: int32 [16], P('tm'), may hold values from 0 to 49, as said below
- pattern: int32 [16, 16], replicated, may hold values from 0 to 1, as said below
Outputs:
- advanced: bfloat16 [16, 768, 4096], P('tm', 'seq')
- next_cache: bfloat16 [16, 2, 768, 4096], P('tm', None, None, 'seq')
Inputs may be any that keep to these rules, and one draw needn't show every extreme that they name: pattern[i][0] is 1 for every i, and pattern[i][j] is 0 where j > i. noise_step[0] is 0, noise_step[15] is 49, and all 16 values are distinct.
All inputs are finite; a program needn't handle non-finite values.
Results may differ from a plain program's by a relative error of at most 0.0036.
Values may be sent and summed in bfloat16 or wider, within the bound.
A program may use at most 64 MiB of HBM per device.

v0:
```python
import math

import jax
import jax.numpy as jnp
from jax import lax
from jax.sharding import PartitionSpec as P

HD = 128


def sent_together(arrays, axis, dim, along):
    ends, at = ([], 0)
    for a in arrays[:-1]:
        at += a.shape[along]
        ends.append(at)
    both = jnp.concatenate(arrays, axis=along)
    return tuple(jnp.split(lax.all_gather(both, axis, axis=dim, tiled=True), ends, axis=along))


def shifted(block, axis, distance):
    devices = range(lax.axis_size(axis))
    route = [(i - distance, i) for i in devices if i - distance in devices]
    return lax.ppermute(block, axis, route)


def absorb(state, query_heads, key_piece, value_piece, scale_factor):
    accum, totals, highest = state
    row_count, head_count, head_dim = query_heads.shape
    key_heads = key_piece.reshape(key_piece.shape[0], head_count, head_dim)
    value_heads = value_piece.reshape(value_piece.shape[0], head_count, head_dim)
    scores = (
        jnp.einsum("qhd,khd->qhk", query_heads, key_heads, preferred_element_type=jnp.float32)
        * scale_factor
    )
    raised = jnp.maximum(highest, jnp.max(scores, axis=-1))
    fade = jnp.exp(highest - raised)
    weights = jnp.exp(scores - raised[..., None])
    totals = totals * fade + jnp.sum(weights, axis=-1)
    accum = accum * fade[..., None] + jnp.einsum(
        "qhk,khd->qhd",
        weights.astype(jnp.bfloat16),
        value_heads,
        preferred_element_type=jnp.float32,
    )
    return (accum, totals, raised)


def body(queries, keys_proj, values, hidden, fresh_latent, gate_table, noise_step, pattern):
    group_index = lax.axis_index("tm")
    final_index = lax.axis_size("tm") - 1
    query_tok, key_tok, value_tok = (
        lax.all_to_all(queries[0], "seq", split_axis=1, concat_axis=0, tiled=True),
        lax.all_to_all(keys_proj[0], "seq", split_axis=1, concat_axis=0, tiled=True),
        lax.all_to_all(values[0], "seq", split_axis=1, concat_axis=0, tiled=True),
    )
    row_count, local_width = query_tok.shape
    head_count = local_width // HD
    query_heads = query_tok.reshape(row_count, head_count, HD)
    scale_factor = 1.0 / math.sqrt(HD)
    reach = lax.dynamic_index_in_dim(pattern, group_index, 0, keepdims=False)
    start_state = (
        jnp.zeros((row_count, head_count, HD), jnp.float32),
        jnp.zeros((row_count, head_count), jnp.float32),
        jnp.full((row_count, head_count), -1e30, jnp.float32),
    )

    def take_group(state, key_block, value_block, source, allowed):

        def use_block(current):
            return absorb(current, query_heads, key_block, value_block, scale_factor)

        def skip_block(current):
            return current

        safe_source = jnp.clip(source, 0, reach.shape[0] - 1)
        flag = allowed & (reach[safe_source] > 0)
        return lax.cond(flag, use_block, skip_block, state)

    state = start_state
    key_piece, value_piece = sent_together((key_tok, value_tok), "tm", 0, 1)
    count = key_piece.shape[0] // row_count
    key_blocks = key_piece.reshape(count, row_count, local_width)
    value_blocks = value_piece.reshape(count, row_count, local_width)
    offsets = jnp.arange(count, dtype=jnp.int32)
    key_blocks, value_blocks, offsets = (key_blocks, value_blocks, offsets)

    def one_block(current, inputs):
        key_block, value_block, source = inputs
        return (take_group(current, key_block, value_block, source, source >= 0), None)

    state, unused = lax.scan(one_block, state, (key_blocks, value_blocks, offsets))
    cache_keys, cache_values = shifted((key_tok, value_tok), "tm", -1)
    accum, totals, highest = state
    attended_head = (accum / totals[..., None]).reshape(row_count, local_width).astype(jnp.bfloat16)
    attended = lax.all_to_all(attended_head, "seq", split_axis=0, concat_axis=1, tiled=True)
    gate_row = lax.dynamic_index_in_dim(gate_table, noise_step[0], 0, keepdims=False)
    updated = (
        hidden[0].astype(jnp.float32) + gate_row[None, :] * attended.astype(jnp.float32)
    ).astype(jnp.bfloat16)
    moved = shifted(updated, "tm", -1)
    advanced = jnp.where(group_index == final_index, fresh_latent, moved)[None]
    next_cache = jnp.stack([cache_keys, cache_values], axis=0)[None]
    return (advanced, next_cache)


def solution(mesh):
    placed = (
        P("tm", "seq", None),
        P("tm", "seq", None),
        P("tm", "seq", None),
        P("tm", "seq", None),
        P("seq", None),
        P(),
        P("tm"),
        P(),
    )
    return jax.shard_map(
        body,
        mesh=mesh,
        in_specs=placed,
        out_specs=(P("tm", "seq", None), P("tm", None, None, "seq")),
        check_vma=False,
    )
```

profile of v0, /device:TPU:59, one launch (start us, length us, event | category | flops | bytes accessed | tf_op | source)
XLA Modules:
  0.0 339.8 jit_solution(10792788455616825555)
XLA Ops:
  7.2 1.1 copy.28
  8.3 0.8 copy.22
  9.0 14.7 %all-to-all-start = ((bf16[24,32,128]{2,0,1:T(8,128)(2,1)}), bf16[24,32,128]{2,0,1:T(8,128)(2,1)S(1)}, u32[]{:S(2)}, u32[]{:S(2)}) async-start(bf16[24,32,128]{2,0,1:T(8,128)(2,1)} %copy.22), calls=%async_computation | async-start | bytes 393216 | tf_op jit(solution)/shard_map/all_to_all | solution.py:53
  23.7 1.0 copy.29
  24.8 11.5 %all-to-all-done = bf16[24,32,128]{2,0,1:T(8,128)(2,1)S(1)} async-done(((bf16[24,32,128]{2,0,1:T(8,128)(2,1)}), bf16[24,32,128]{2,0,1:T(8,128)(2,1)S(1)}, u32[]{:S(2)}, u32[]{:S(2)}) %all-to-all-start) | async-done | bytes 196640 | tf_op jit(solution)/shard_map/all_to_all | solution.py:53
  36.3 21.3 %all_to_all.64 = bf16[24,32,128]{2,0,1:T(8,128)(2,1)S(1)} all-to-all(bf16[24,32,128]{2,0,1:T(8,128)(2,1)S(1)} %copy.23), channel_id=1, replica_groups=mesh['tm'=16,'seq'=32] {'seq'}, dimensions={1} | all-to-all | bytes 393216 | tf_op jit(solution)/shard_map/all_to_all | solution.py:54
  57.6 0.8 pad_maximum_fusion
  58.5 0.8 copy.24
  59.2 8.6 %all-to-all-start.2 = ((bf16[24,32,128]{2,0,1:T(8,128)(2,1)}), bf16[24,32,128]{2,0,1:T(8,128)(2,1)S(1)}, u32[]{:S(2)}, u32[]{:S(2)}) async-start(bf16[24,32,128]{2,0,1:T(8,128)(2,1)} %copy.24), calls=%async_computation.2 | async-start | bytes 393216 | tf_op jit(solution)/shard_map/all_to_all | solution.py:52
  67.9 0.7 dynamic-slice_bitcast_fusion
  68.5 127.8 %all-gather.2.cloned.1.call-done = bf16[12288,256]{1,0:T(8,128)(2,1)} async-done(((bf16[768,256]{1,0:T(8,128)(2,1)}), bf16[12288,256]{1,0:T(8,128)(2,1)}) %all-gather.2.cloned.1.call-update) | async-done | bytes 6291472 | tf_op jit(solution)/shard_map/all_gather | solution.py:17
  196.3 4.7 %fusion.20 = (bf16[12288,128]{1,0:T(8,128)(2,1)}, bf16[12288,128]{1,0:T(8,128)(2,1)}) fusion(bf16[12288,256]{1,0:T(8,128)(2,1)} %all-gather.2.cloned.1.call-done), kind=kLoop, calls=%fused_computation.33 | loop fusion | bytes 12582912 | tf_op jit(solution)/shard_map/split | solution.py:17
  201.1 69.8 %while.14 = (s32[]{:T(128)}, f32[768,1,128]{0,2,1:T(8,128)S(1)}, f32[768,1]{0,1:T(1,128)S(1)}, f32[768,1]{0,1:T(1,128)S(1)}, s32[16]{0:T(128)S(1)}, /*index=5*/s...) while((s32[]{:T(128)}, f32[768,1,128]{0,2,1:T(8,128)S(1)}, ...), condition=%wide.region_5.6_spmd, body=%wide.region_0.5_spmd.sunk | while | flops 306907392 | bytes 8507695 | solution.py:91
  201.2 0.6 dynamic_slice.48
  202.4 0.7 dynamic_slice.49
  204.4 3.5 %conditional.2 = ((f32[768,1,128]{0,2,1:T(8,128)S(1)}, f32[768,1]{0,1:T(1,128)S(1)}, f32[768,1]{0,1:T(1,128)S(1)})) conditional(s32[]{:T(128)} %bitcast.84, (f32[768,1,128]{0,2,1:T(8,128)S(1)}, f32[768,1]{0,1:T(1,128)S(1)}, f32[768,1]{0,1:T(1,128)S(1)}) %tuple.39, (bf16[16,768,128]{2,1,0:T(8,128)(2,1)}, s32[]{:T(128)}, ...), branch_computations={%region_1.1_spmd, %region_2.4_spmd} | conditional | flops 306907392 | bytes 8507424 | solution.py:77
  204.4 1.4 multiply_reduce_fusion
  206.3 1.6 fusion.3
  207.9 0.6 dynamic_slice.48
  209.2 0.7 dynamic_slice.49
  211.2 0.6 dynamic_slice.48
  212.4 0.7 dynamic_slice.49
  214.4 3.5 %conditional.2 = ((f32[768,1,128]{0,2,1:T(8,128)S(1)}, f32[768,1]{0,1:T(1,128)S(1)}, f32[768,1]{0,1:T(1,128)S(1)})) conditional(s32[]{:T(128)} %bitcast.84, (f32[768,1,128]{0,2,1:T(8,128)S(1)}, f32[768,1]{0,1:T(1,128)S(1)}, f32[768,1]{0,1:T(1,128)S(1)}) %tuple.39, (bf16[16,768,128]{2,1,0:T(8,128)(2,1)}, s32[]{:T(128)}, ...), branch_computations={%region_1.1_spmd, %region_2.4_spmd} | conditional | flops 306907392 | bytes 8507424 | solution.py:77
  214.4 1.4 multiply_reduce_fusion
  216.3 1.6 fusion.3
  217.9 0.6 dynamic_slice.48
  219.2 0.7 dynamic_slice.49
  221.2 3.5 %conditional.2 = ((f32[768,1,128]{0,2,1:T(8,128)S(1)}, f32[768,1]{0,1:T(1,128)S(1)}, f32[768,1]{0,1:T(1,128)S(1)})) conditional(s32[]{:T(128)} %bitcast.84, (f32[768,1,128]{0,2,1:T(8,128)S(1)}, f32[768,1]{0,1:T(1,128)S(1)}, f32[768,1]{0,1:T(1,128)S(1)}) %tuple.39, (bf16[16,768,128]{2,1,0:T(8,128)(2,1)}, s32[]{:T(128)}, ...), branch_computations={%region_1.1_spmd, %region_2.4_spmd} | conditional | flops 306907392 | bytes 8507424 | solution.py:77
  221.2 1.4 multiply_reduce_fusion
  223.1 1.6 fusion.3
  224.7 0.6 dynamic_slice.48
  225.9 0.7 dynamic_slice.49
  227.9 3.5 %conditional.2 = ((f32[768,1,128]{0,2,1:T(8,128)S(1)}, f32[768,1]{0,1:T(1,128)S(1)}, f32[768,1]{0,1:T(1,128)S(1)})) conditional(s32[]{:T(128)} %bitcast.84, (f32[768,1,128]{0,2,1:T(8,128)S(1)}, f32[768,1]{0,1:T(1,128)S(1)}, f32[768,1]{0,1:T(1,128)S(1)}) %tuple.39, (bf16[16,768,128]{2,1,0:T(8,128)(2,1)}, s32[]{:T(128)}, ...), branch_computations={%region_1.1_spmd, %region_2.4_spmd} | conditional | flops 306907392 | bytes 8507424 | solution.py:77
  228.0 1.4 multiply_reduce_fusion
  229.8 1.6 fusion.3
  231.5 0.6 dynamic_slice.48
  232.7 0.7 dynamic_slice.49
  234.7 3.5 %conditional.2 = ((f32[768,1,128]{0,2,1:T(8,128)S(1)}, f32[768,1]{0,1:T(1,128)S(1)}, f32[768,1]{0,1:T(1,128)S(1)})) conditional(s32[]{:T(128)} %bitcast.84, (f32[768,1,128]{0,2,1:T(8,128)S(1)}, f32[768,1]{0,1:T(1,128)S(1)}, f32[768,1]{0,1:T(1,128)S(1)}) %tuple.39, (bf16[16,768,128]{2,1,0:T(8,128)(2,1)}, s32[]{:T(128)}, ...), branch_computations={%region_1.1_spmd, %region_2.4_spmd} | conditional | flops 306907392 | bytes 8507424 | solution.py:77
  234.7 1.4 multiply_reduce_fusion
  236.6 1.6 fusion.3
  238.2 0.6 dynamic_slice.48
  239.5 0.7 dynamic_slice.49
  241.5 0.6 dynamic_slice.48
  242.7 0.7 dynamic_slice.49
  244.8 0.6 dynamic_slice.48
  246.0 0.7 dynamic_slice.49
  249.3 0.7 dynamic_slice.49
  252.6 0.7 dynamic_slice.49
  255.8 0.7 dynamic_slice.49
  259.1 0.7 dynamic_slice.49
  261.1 0.6 dynamic_slice.48
  262.4 0.7 dynamic_slice.49
  265.7 0.7 dynamic_slice.49
  268.9 0.7 dynamic_slice.49
  271.2 0.9 divide_convert_fusion
  272.0 16.3 %all-to-all-start.3 = ((bf16[32,24,128]{2,1,0:T(8,128)(2,1)}), bf16[32,24,128]{2,1,0:T(8,128)(2,1)S(1)}, u32[]{:S(2)}, u32[]{:S(2)}) async-start(bf16[32,24,128]{2,1,0:T(8,128)(2,1)} %bitcast.22), calls=%async_computation.3 | async-start | bytes 393216 | tf_op jit(solution)/shard_map/all_to_all | solution.py:95
  289.0 9.7 %collective-permute-start.1 = (bf16[768,128]{1,0:T(8,128)(2,1)S(1)}, bf16[768,128]{1,0:T(8,128)(2,1)S(1)}, u32[]{:S(2)}, u32[]{:S(2)}) collective-permute-start(bf16[768,128]{1,0:T(8,128)(2,1)S(1)} %bitcast.95), channel_id=1, source_target_pairs={{32,0},{64,32},{96,64},{128,96},{160,128},{192,160},{224,192},{256... | collective-permute-start | bytes 589832 | tf_op jit(solution)/shard_map/ppermute | solution.py:23
  298.7 1.9 collective-permute-start.2
  300.7 9.1 %collective-permute-start = (bf16[24,4096]{1,0:T(8,128)(2,1)S(1)}, bf16[24,4096]{1,0:T(8,128)(2,1)S(1)}, u32[]{:S(2)}, u32[]{:S(2)}) collective-permute-start(bf16[24,4096]{1,0:T(8,128)(2,1)S(1)} %fusion.19), channel_id=1, source_target_pairs={{32,0},{64,32},{96,64},{128,96},{160,128},{192,160},{224,192},{256... | collective-permute-start | bytes 589832 | tf_op jit(solution)/shard_map/ppermute | solution.py:23
  309.8 3.9 %collective-permute-done.1 = bf16[768,128]{1,0:T(8,128)(2,1)S(1)} collective-permute-done((bf16[768,128]{1,0:T(8,128)(2,1)S(1)}, bf16[768,128]{1,0:T(8,128)(2,1)S(1)}, u32[]{:S(2)}, u32[]{:S(2)}) %collective-permute-start.1) | collective-permute-done | bytes 196640 | tf_op jit(solution)/shard_map/ppermute | solution.py:23
  313.8 16.4 %collective-permute-done.2 = bf16[768,128]{1,0:T(8,128)(2,1)S(1)} collective-permute-done((bf16[768,128]{1,0:T(8,128)(2,1)S(1)}, bf16[768,128]{1,0:T(8,128)(2,1)S(1)}, u32[]{:S(2)}, u32[]{:S(2)}) %collective-permute-start.2) | collective-permute-done | bytes 196640 | tf_op jit(solution)/shard_map/ppermute | solution.py:23
  330.1 0.8 maximum_bitcast_fusion
  330.9 1.3 collective-permute-done
  332.3 0.7 select_bitcast_fusion
  (59 shorter events, 6.5 us)
Async XLA Ops:
  7.2 281.8 %copy-start = (f32[50,4096]{1,0:T(8,128)S(1)}, f32[50,4096]{1,0:T(8,128)}, u32[]{:S(2)}) copy-start(f32[50,4096]{1,0:T(8,128)} %param.17) | copy-start | bytes 2457604
  7.2 51.2 %copy-start.1 = (bf16[1,24,4096]{2,1,0:T(8,128)(2,1)S(1)}, bf16[1,24,4096]{2,1,0:T(8,128)(2,1)}, u32[]{:S(2)}) copy-start(bf16[1,24,4096]{2,1,0:T(8,128)(2,1)} %param.12) | copy-start | bytes 589828
  9.0 27.3 %all-to-all-start = ((bf16[24,32,128]{2,0,1:T(8,128)(2,1)}), bf16[24,32,128]{2,0,1:T(8,128)(2,1)S(1)}, u32[]{:S(2)}, u32[]{:S(2)}) async-start(bf16[24,32,128]{2,0,1:T(8,128)(2,1)} %copy.22), calls=%async_computation | async-start | bytes 393216 | tf_op jit(solution)/shard_map/all_to_all | solution.py:53
  23.7 172.7 %all-gather.2.cloned.1.call-start = ((), (), s32[]{:S(2)}) async-start(), calls=%async_computation.4 | async-start | bytes 6684672 | tf_op jit(solution)/shard_map/all_gather | solution.py:17
  59.2 141.9 %all-to-all-start.2 = ((bf16[24,32,128]{2,0,1:T(8,128)(2,1)}), bf16[24,32,128]{2,0,1:T(8,128)(2,1)S(1)}, u32[]{:S(2)}, u32[]{:S(2)}) async-start(bf16[24,32,128]{2,0,1:T(8,128)(2,1)} %copy.24), calls=%async_computation.2 | async-start | bytes 393216 | tf_op jit(solution)/shard_map/all_to_all | solution.py:52
  201.1 99.5 %copy-start.2 = (bf16[1,24,4096]{2,1,0:T(8,128)(2,1)S(1)}, bf16[1,24,4096]{2,1,0:T(8,128)(2,1)}, u32[]{:S(2)}) copy-start(bf16[1,24,4096]{2,1,0:T(8,128)(2,1)} %param.15) | copy-start | bytes 589828
  271.0 61.3 %copy-start.3 = (bf16[24,4096]{1,0:T(8,128)(2,1)S(1)}, bf16[24,4096]{1,0:T(8,128)(2,1)}, u32[]{:S(2)}) copy-start(bf16[24,4096]{1,0:T(8,128)(2,1)} %param.16) | copy-start | bytes 589828
  272.0 28.6 %all-to-all-start.3 = ((bf16[32,24,128]{2,1,0:T(8,128)(2,1)}), bf16[32,24,128]{2,1,0:T(8,128)(2,1)S(1)}, u32[]{:S(2)}, u32[]{:S(2)}) async-start(bf16[32,24,128]{2,1,0:T(8,128)(2,1)} %bitcast.22), calls=%async_computation.3 | async-start | bytes 393216 | tf_op jit(solution)/shard_map/all_to_all | solution.py:95
  289.0 24.8 %collective-permute-start.1 = (bf16[768,128]{1,0:T(8,128)(2,1)S(1)}, bf16[768,128]{1,0:T(8,128)(2,1)S(1)}, u32[]{:S(2)}, u32[]{:S(2)}) collective-permute-start(bf16[768,128]{1,0:T(8,128)(2,1)S(1)} %bitcast.95), channel_id=1, source_target_pairs={{32,0},{64,32},{96,64},{128,96},{160,128},{192,160},{224,192},{256... | collective-permute-start | bytes 589832 | tf_op jit(solution)/shard_map/ppermute | solution.py:23
  298.7 31.4 %collective-permute-start.2 = (bf16[768,128]{1,0:T(8,128)(2,1)S(1)}, bf16[768,128]{1,0:T(8,128)(2,1)S(1)}, u32[]{:S(2)}, u32[]{:S(2)}) collective-permute-start(bf16[768,128]{1,0:T(8,128)(2,1)S(1)} %bitcast.97), channel_id=1, source_target_pairs={{32,0},{64,32},{96,64},{128,96},{160,128},{192,160},{224,192},{256... | collective-permute-start | bytes 589832 | tf_op jit(solution)/shard_map/ppermute | solution.py:23
  300.7 31.5 %collective-permute-start = (bf16[24,4096]{1,0:T(8,128)(2,1)S(1)}, bf16[24,4096]{1,0:T(8,128)(2,1)S(1)}, u32[]{:S(2)}, u32[]{:S(2)}) collective-permute-start(bf16[24,4096]{1,0:T(8,128)(2,1)S(1)} %fusion.19), channel_id=1, source_target_pairs={{32,0},{64,32},{96,64},{128,96},{160,128},{192,160},{224,192},{256... | collective-permute-start | bytes 589832 | tf_op jit(solution)/shard_map/ppermute | solution.py:23
Sparse Core Ops, SparseCore 0:
  58.5 137.7 all-gather.1
where the time goes:
time: 341 us; the launch traced here: 340 us
  waiting for transfers between devices  161 us (47%)
  starting transfers between devices  60.3 us (18%)
  loops' own time  32.6 us (10%)
  local copies, waits for them, and re-layouts  29.2 us (9%)
  blocking collectives  21.3 us (6%)
  matrix products  14.9 us (4%)
  between operations  14.9 us (4%)
  other arithmetic  5.54 us (2%)
    all_gather x1, waiting for transfers between devices, sent_together(): lax.all_gather(both, axis, axis=dim, tiled=True)  128 us
    another operation x1, loops' own time, body(): lax.scan(one_block, state, (key_blocks, value_blocks, offsets))  32.3 us
    ppermute x3, waiting for transfers between devices, shifted(): return lax.ppermute(block, axis, route)  21.6 us
    all_to_all x1, blocking collectives, body(): lax.all_to_all(values[0], 'seq', split_axis=1, concat_axis=0, tiled=True)  21.3 us
    ppermute x3, starting transfers between devices, shifted(): return lax.ppermute(block, axis, route)  20.7 us
    all_to_all x1, starting transfers between devices, body(): lax.all_to_all(attended_head, 'seq', split_axis=0, concat_axis=1, tiled=T...  16.3 us
    all_to_all x1, starting transfers between devices, body(): lax.all_to_all(keys_proj[0], 'seq', split_axis=1, concat_axis=0, tiled=True)  14.7 us
    all_to_all x1, waiting for transfers between devices, body(): lax.all_to_all(keys_proj[0], 'seq', split_axis=1, concat_axis=0, tiled=True)  11.5 us
  transfers between devices with their start and end apart: 7, of which 5 were waited for; matrix products, arithmetic and copies ran while one was open for 2% of the time, Pallas kernels for 0%

commit v1 on v0

v1 whole, which is shorter than its diff:
```python
import functools
import math

import jax
import jax.numpy as jnp
from jax import lax
from jax.experimental import pallas as pl
from jax.experimental.pallas import tpu as pltpu
from jax.sharding import PartitionSpec as P

HD = 128
NG = 16
NS = 32
TOK = 24
ROWS = 768
MESH = pl.DeviceIdType.MESH
LOG2E = math.log2(math.e)


def remote(src, dst, send_sem, recv_sem, g, s):
    return pltpu.make_async_remote_copy(
        src_ref=src,
        dst_ref=dst,
        send_sem=send_sem,
        recv_sem=recv_sem,
        device_id=(g, s),
        device_id_type=MESH,
    )


def drain(ref, sem):
    pltpu.make_async_copy(ref, ref, sem).wait()


def signal(sem, g, s):
    pl.semaphore_signal(sem, inc=1, device_id=(g, s), device_id_type=MESH)


def exchange_kernel(
    k_ref,
    v_ref,
    q_ref,
    hid_ref,
    gate_ref,
    kv_ref,
    qh_ref,
    hid_next_ref,
    gate_next_ref,
    p1_send,
    p1_recv,
    q_send,
    q_recv,
    ring_send,
    ring_recv,
    relay_send,
    relay_recv,
    sib_send,
    sib_recv,
    hid_send,
    hid_recv,
):
    g = lax.axis_index("tm")
    s = lax.axis_index("seq")
    z = g // 8
    y = (g % 8) // 2
    c = g % 2
    right = (y + 1) % 4
    left = (y + 3) % 4
    across = (y + 2) % 4
    partner = (g + 8) % 16
    g_right = 8 * z + 2 * right + c
    g_left = 8 * z + 2 * left + c
    g_sib = 8 * z + 2 * y + 1 - c

    barrier = pltpu.get_barrier_semaphore()

    def greet_seq(i, carry):
        signal(barrier, g, (s + i) % NS)
        return carry

    def greet_partner(i, carry):
        signal(barrier, partner, (s + i) % NS)
        return carry

    lax.fori_loop(1, NS, greet_seq, 0)
    lax.fori_loop(0, NS, greet_partner, 0)
    signal(barrier, g_right, s)
    signal(barrier, g_left, s)
    signal(barrier, g_sib, s)

    @pl.when(g == 7)
    def _():
        lax.fori_loop(0, NS, lambda i, x: (signal(barrier, 8, (s + i) % NS), x)[1], 0)

    @pl.when(g == 8)
    def _():
        lax.fori_loop(0, NS, lambda i, x: (signal(barrier, 7, (s + i) % NS), x)[1], 0)

    @pl.when((c == 1) & (g < 15) & (g != 7))
    def _():
        signal(barrier, g + 1, s)

    @pl.when((c == 0) & (g > 0) & (g != 8))
    def _():
        signal(barrier, g - 1, s)

    extra = jnp.where(
        (g == 7) | (g == 8),
        NS,
        jnp.where((g == 0) | (g == 15), 0, 1),
    )
    pl.semaphore_wait(barrier, NS - 1 + NS + 3 + extra)

    row = pl.multiple_of(s * TOK, 8)

    def near(src, dst, send_sem, recv_sem, h):
        cols = pl.ds(pl.multiple_of(h * HD, HD), HD)
        remote(src.at[:, cols], dst.at[pl.ds(row, TOK)], send_sem, recv_sem, g, h).start()

    for kind, src in ((0, k_ref), (1, v_ref)):
        own = pl.ds(pl.multiple_of(s * HD, HD), HD)
        pltpu.make_async_copy(
            src.at[:, own], kv_ref.at[g, kind, pl.ds(row, TOK)], p1_recv.at[0, kind]
        ).start()

        def send_low(i, carry, kind=kind, src=src):
            h = (s + i) % NS
            cols = pl.ds(pl.multiple_of(h * HD, HD), HD)
            remote(
                src.at[:, cols],
                kv_ref.at[g, kind, pl.ds(row, TOK)],
                p1_send.at[1, kind],
                p1_recv.at[1, kind],
                g + 8,
                h,
            ).start()
            return carry

        def send_near(i, carry, kind=kind, src=src):
            h = (s + i) % NS
            near(src, kv_ref.at[g, kind], p1_send.at[0, kind], p1_recv.at[0, kind], h)
            return carry

        def send_down(i, carry, kind=kind, src=src):
            h = (s + i) % NS
            cols = pl.ds(pl.multiple_of(h * HD, HD), HD)
            remote(
                src.at[:, cols],
                kv_ref.at[8, kind, pl.ds(row, TOK)],
                p1_send.at[1, kind],
                p1_recv.at[1, kind],
                7,
                h,
            ).start()
            return carry

        @pl.when(z == 0)
        def _(send_low=send_low):
            lax.fori_loop(0, NS, send_low, 0)

        lax.fori_loop(1, NS, send_near, 0)

        @pl.when(g == 8)
        def _(send_down=send_down):
            lax.fori_loop(0, NS, send_down, 0)

    own = pl.ds(pl.multiple_of(s * HD, HD), HD)
    pltpu.make_async_copy(q_ref.at[:, own], qh_ref.at[pl.ds(row, TOK)], q_recv).start()

    def send_q(i, carry):
        near(q_ref, qh_ref, q_send, q_recv, (s + i) % NS)
        return carry

    lax.fori_loop(1, NS, send_q, 0)

    @pl.when(g > 0)
    def _():
        remote(hid_ref, hid_next_ref, hid_send.at[0], hid_recv.at[0], g - 1, s).start()
        remote(gate_ref, gate_next_ref, hid_send.at[1], hid_recv.at[1], g - 1, s).start()

    def slot(ab, yy, cc):
        return 8 * z * (1 - ab) + 2 * yy + cc

    def ring(kind, ab, way, target):
        piece = kv_ref.at[slot(ab, y, c), kind]
        return remote(piece, piece, ring_send.at[kind, ab, way], ring_recv.at[kind, ab, way], target, s)

    def relay(kind, ab):
        owner = left if kind == 0 else right
        target = g_right if kind == 0 else g_left
        piece = kv_ref.at[slot(ab, owner, c), kind]
        return remote(piece, piece, relay_send.at[kind, ab], relay_recv.at[kind, ab], target, s)

    def sib(kind, ab, yy):
        piece = kv_ref.at[slot(ab, yy, c), kind]
        return remote(piece, piece, sib_send.at[kind, ab, yy], sib_recv.at[kind, ab, yy], g_sib, s)

    for kind in (0, 1):

        def open_own(ab, carry, kind=kind):
            drain(kv_ref.at[slot(ab, y, c), kind], p1_recv.at[ab, kind])
            ring(kind, ab, 0, g_right).start()
            ring(kind, ab, 1, g_left).start()
            sib(kind, ab, y).start()
            return carry

        def open_ring(ab, carry, kind=kind):
            drain(kv_ref.at[slot(ab, left, c), kind], ring_recv.at[kind, ab, 0])
            if kind == 0:
                relay(kind, ab).start()
            sib(kind, ab, left).start()
            drain(kv_ref.at[slot(ab, right, c), kind], ring_recv.at[kind, ab, 1])
            if kind == 1:
                relay(kind, ab).start()
            sib(kind, ab, right).start()
            return carry

        def open_across(ab, carry, kind=kind):
            drain(kv_ref.at[slot(ab, across, c), kind], relay_recv.at[kind, ab])
            sib(kind, ab, across).start()
            return carry

        lax.fori_loop(0, z + 1, open_own, 0)
        lax.fori_loop(0, z + 1, open_ring, 0)
        lax.fori_loop(0, z + 1, open_across, 0)

    for kind in (0, 1):

        @pl.when(g == 7)
        def _(kind=kind):
            drain(kv_ref.at[8, kind], p1_recv.at[1, kind])

        def close(ab, carry, kind=kind):
            def close_sib(yy, inner):
                drain(kv_ref.at[slot(ab, yy, 1 - c), kind], sib_recv.at[kind, ab, yy])
                sib(kind, ab, yy).wait_send()
                return inner

            lax.fori_loop(0, 4, close_sib, 0)
            ring(kind, ab, 0, g_right).wait_send()
            ring(kind, ab, 1, g_left).wait_send()
            relay(kind, ab).wait_send()
            return carry

        lax.fori_loop(0, z + 1, close, 0)
        drain(kv_ref.at[g, kind, pl.ds(0, ROWS - TOK)], p1_send.at[0, kind])

        @pl.when((z == 0) | (g == 8))
        def _(kind=kind):
            drain(kv_ref.at[g, kind], p1_send.at[1, kind])

    drain(qh_ref, q_recv)
    drain(qh_ref.at[pl.ds(0, ROWS - TOK)], q_send)

    @pl.when(g > 0)
    def _():
        remote(hid_ref, hid_next_ref, hid_send.at[0], hid_recv.at[0], g - 1, s).wait_send()
        remote(gate_ref, gate_next_ref, hid_send.at[1], hid_recv.at[1], g - 1, s).wait_send()

    @pl.when(g < 15)
    def _():
        drain(hid_next_ref, hid_recv.at[0])
        drain(gate_next_ref, hid_recv.at[1])


def exchange(keys, values, queries, hidden, gate_row):
    vmem = pl.BlockSpec(memory_space=pltpu.VMEM)
    hbm = pl.BlockSpec(memory_space=pl.ANY)
    dma = pltpu.SemaphoreType.DMA
    return pl.pallas_call(
        exchange_kernel,
        out_shape=(
            jax.ShapeDtypeStruct((NG, 2, ROWS, HD), jnp.bfloat16),
            jax.ShapeDtypeStruct((ROWS, HD), jnp.bfloat16),
            jax.ShapeDtypeStruct(hidden.shape, jnp.bfloat16),
            jax.ShapeDtypeStruct(gate_row.shape, jnp.float32),
        ),
        in_specs=[vmem] * 5,
        out_specs=(hbm,) * 4,
        scratch_shapes=[
            dma((2, 2)),
            dma((2, 2)),
            dma,
            dma,
            dma((2, 2, 2)),
            dma((2, 2, 2)),
            dma((2, 2)),
            dma((2, 2)),
            dma((2, 2, 4)),
            dma((2, 2, 4)),
            dma((2,)),
            dma((2,)),
        ],
        compiler_params=pltpu.CompilerParams(collective_id=0, has_side_effects=True),
        name="exchange",
    )(keys, values, queries, hidden, gate_row)


def attend_kernel(pattern_ref, group_ref, q_ref, kv_ref, next_ref, o_ref, cache_ref, acc, high, total):
    j = pl.program_id(0)
    g = group_ref[0]

    @pl.when(j == 0)
    def _():
        acc[...] = jnp.zeros_like(acc)
        total[...] = jnp.zeros_like(total)
        high[...] = jnp.full_like(high, -1e30)
        cache_ref[...] = jnp.where(g < NG - 1, next_ref[0], jnp.zeros_like(cache_ref))

    @pl.when((j <= g) & (pattern_ref[g, j] > 0))
    def _():
        keys = kv_ref[0, 0]
        values_t = kv_ref[0, 1].T
        width = 256
        for at in range(0, ROWS, width):
            span = pl.ds(at, width)
            scores = lax.dot_general(
                keys, q_ref[span, :], (((1,), (1,)), ((), ())), preferred_element_type=jnp.float32
            ) * (LOG2E / math.sqrt(HD))
            before = high[:, span]
            raised = jnp.maximum(before, jnp.max(scores, axis=0, keepdims=True))
            fade = jnp.exp2(before - raised)
            probs = jnp.exp2(scores - raised)
            high[:, span] = raised
            total[:, span] = total[:, span] * fade + jnp.sum(probs, axis=0, keepdims=True)
            acc[:, span] = acc[:, span] * fade + jnp.dot(
                values_t, probs.astype(jnp.bfloat16), preferred_element_type=jnp.float32
            )

    @pl.when(j == NG - 1)
    def _():
        o_ref[...] = (acc[...] / total[...]).T.astype(jnp.bfloat16)


def attend(pattern, group, qh, kv):
    grid_spec = pltpu.PrefetchScalarGridSpec(
        num_scalar_prefetch=2,
        grid=(NG,),
        in_specs=[
            pl.BlockSpec((ROWS, HD), lambda j, p, g: (0, 0)),
            pl.BlockSpec((1, 2, ROWS, HD), lambda j, p, g: (jnp.minimum(j, g[0]), 0, 0, 0)),
            pl.BlockSpec((1, 2, ROWS, HD), lambda j, p, g: (jnp.minimum(g[0] + 1, NG - 1), 0, 0, 0)),
        ],
        out_specs=[
            pl.BlockSpec((ROWS, HD), lambda j, p, g: (0, 0)),
            pl.BlockSpec((2, ROWS, HD), lambda j, p, g: (0, 0, 0)),
        ],
        scratch_shapes=[
            pltpu.VMEM((HD, ROWS), jnp.float32),
            pltpu.VMEM((1, ROWS), jnp.float32),
            pltpu.VMEM((1, ROWS), jnp.float32),
        ],
    )
    return pl.pallas_call(
        attend_kernel,
        out_shape=(
            jax.ShapeDtypeStruct((ROWS, HD), jnp.bfloat16),
            jax.ShapeDtypeStruct((2, ROWS, HD), jnp.bfloat16),
        ),
        grid_spec=grid_spec,
        name="attend",
    )(pattern, group, qh, kv, kv)


def return_kernel(o_ref, hid_ref, gate_ref, fresh_ref, out_ref, landed, send_sem, recv_sem):
    g = lax.axis_index("tm")
    s = lax.axis_index("seq")
    barrier = pltpu.get_barrier_semaphore()

    @pl.when(g > 0)
    def _():
        lax.fori_loop(0, NS, lambda i, x: (signal(barrier, g - 1, (s + i) % NS), x)[1], 0)

    @pl.when(g < NG - 1)
    def _():
        lax.fori_loop(0, NS, lambda i, x: (signal(barrier, g + 1, (s + i) % NS), x)[1], 0)

    pl.semaphore_wait(barrier, jnp.where((g == 0) | (g == NG - 1), NS, 2 * NS))
    cols = pl.ds(pl.multiple_of(s * HD, HD), HD)

    @pl.when(g > 0)
    def _():
        def send(i, carry):
            t = (s + i) % NS
            remote(
                o_ref.at[pl.ds(pl.multiple_of(t * TOK, 8), TOK)],
                landed.at[:, cols],
                send_sem,
                recv_sem,
                g - 1,
                t,
            ).start()
            return carry

        lax.fori_loop(0, NS, send, 0)
        drain(o_ref, send_sem)

    @pl.when(g < NG - 1)
    def _():
        drain(landed, recv_sem)
        out_ref[...] = (
            hid_ref[...].astype(jnp.float32) + gate_ref[...] * landed[...].astype(jnp.float32)
        ).astype(jnp.bfloat16)

    @pl.when(g == NG - 1)
    def _():
        out_ref[...] = fresh_ref[...]


def give_back(o, hid_next, gate_next, fresh):
    vmem = pl.BlockSpec(memory_space=pltpu.VMEM)
    dma = pltpu.SemaphoreType.DMA
    return pl.pallas_call(
        return_kernel,
        out_shape=jax.ShapeDtypeStruct(fresh.shape, jnp.bfloat16),
        in_specs=[vmem] * 4,
        out_specs=vmem,
        scratch_shapes=[pltpu.VMEM(fresh.shape, jnp.bfloat16), dma, dma],
        compiler_params=pltpu.CompilerParams(collective_id=1, has_side_effects=True),
        name="give_back",
    )(o, hid_next, gate_next, fresh)


def body(queries, keys_proj, values, hidden, fresh_latent, gate_table, noise_step, pattern):
    group = lax.axis_index("tm").astype(jnp.int32).reshape(1)
    gate_row = lax.dynamic_slice_in_dim(gate_table, noise_step[0], 1, 0)
    kv, qh, hid_next, gate_next = exchange(keys_proj[0], values[0], queries[0], hidden[0], gate_row)
    attended, next_cache = attend(pattern, group, qh, kv)
    advanced = give_back(attended, hid_next, gate_next, fresh_latent)
    return (advanced[None], next_cache[None])


def solution(mesh):
    placed = (
        P("tm", "seq", None),
        P("tm", "seq", None),
        P("tm", "seq", None),
        P("tm", "seq", None),
        P("seq", None),
        P(),
        P("tm"),
        P(),
    )
    return jax.shard_map(
        body,
        mesh=mesh,
        in_specs=placed,
        out_specs=(P("tm", "seq", None), P("tm", None, None, "seq")),
        check_vma=False,
    )
```

time: 341 us -> 117 us (0.34)
  the two profiles are of different devices: /device:TPU:59 before, /device:TPU:57 now
where the time goes in v1:
time: 117 us; the launch traced here: 118 us
  Pallas kernels  113 us (97%)
  local copies, waits for them, and re-layouts  2.7 us (2%)
  between operations  1.39 us (1%)
    pallas_call x1, Pallas kernels, exchange(): pl.pallas_call(exchange_kernel, out_shape=(jax.ShapeDtypeStruct((NG, 2, R...  72 us
    pallas_call x1, Pallas kernels, give_back(): pl.pallas_call(return_kernel, out_shape=jax.ShapeDtypeStruct(fresh.shape,...  24.7 us
    pallas_call x1, Pallas kernels, attend(): pl.pallas_call(attend_kernel, out_shape=(jax.ShapeDtypeStruct((ROWS, HD),...  16.8 us

profile of v1, /device:TPU:57, one launch (start us, length us, event | category | flops | bytes accessed | tf_op | source)
XLA Modules:
  0.0 117.6 jit_solution(1895077282991911028)
XLA Ops:
  0.6 0.0 copy-start
  1.4 0.5 copy-done
  1.8 0.6 constant_dynamic-slice_fusion.gate_ref
  2.5 72.0 %exchange.1 = (bf16[16,2,768,128]{3,2,1,0:T(8,128)(2,1)}, bf16[768,128]{1,0:T(8,128)(2,1)}, bf16[24,4096]{1,0:T(8,128)(2,1)}, f32[1,4096]{1,0:T(1,128)}) custom-call(bf16[24,4096]{1,0:T(8,128)(2,1)} %bitcast.12, bf16[24,4096]{1,0:T(8,128)(2,1)} %bitcast.13, bf16[24,4096]{1,0:T(8,128)(2,1)} %bitcast.14, bf16[24,4096]{1,0:T(8,128)(2,1)} %bitcast.15, ...), custom_call_target="tpu_custom_call" | custom-call | tf_op jit(solution)/shard_map/exchange/pallas_call | solution.py:270
  74.4 16.8 %attend.1 = (bf16[768,128]{1,0:T(8,128)(2,1)}, bf16[2,768,128]{2,1,0:T(8,128)(2,1)}) custom-call(s32[16,16]{1,0:T(8,128)} %pattern_ref.1, s32[1]{0:T(128)} %bitcast.group_ref, bf16[768,128]{1,0:T(8,128)(2,1)} %get-tuple-element.8.q_ref, bf16[16,2,768,128]{3,2,1,0:T(8,128)(2,1)} %get-tuple-element.9.kv_ref.next_ref, ...), custom_call_target="tpu_custom_call" | custom-call | tf_op jit(solution)/shard_map/attend/pallas_call | solution.py:354
  91.2 24.7 %give_back.1 = bf16[24,4096]{1,0:T(8,128)(2,1)} custom-call(bf16[768,128]{1,0:T(8,128)(2,1)} %get-tuple-element.10.o_ref, bf16[24,4096]{1,0:T(8,128)(2,1)} %get-tuple-element.11.hid_ref, f32[1,4096]{1,0:T(1,128)} %get-tuple-element.12.gate_ref, bf16[24,4096]{1,0:T(8,128)(2,1)} %fresh_ref.1), custom_call_target="tpu_custom_call" | custom-call | tf_op jit(solution)/shard_map/give_back/pallas_call | solution.py:413
  115.9 1.6 %copy.12 = bf16[1,24,4096]{2,1,0:T(8,128)(2,1)} copy(bf16[1,24,4096]{2,1,0:T(8,128)(2,1)} %bitcast.11) | data formatting | bytes 393216
Async XLA Ops:
  0.6 1.2 %copy-start = (f32[50,4096]{1,0:T(8,128)S(1)}, f32[50,4096]{1,0:T(8,128)}, u32[]{:S(2)}) copy-start(f32[50,4096]{1,0:T(8,128)} %param.13) | copy-start | bytes 2457604
